TPU v7x, 32 devices: a whole 2x2x4 slice. The times are simulated.
32 devices in a mesh: row: 4 (over x, core), col: 8 (over z, y).
Axes of the slice: x: 2, y: 2, z: 4, core: 2. Of those that a mesh axis runs over, the one named last changes fastest.
Arguments:
- optical_field: float32 [2, 512, 4096], P(None, 'row', 'col'), may hold values from -6 to 6
- index_panels: bfloat16 [5, 512, 4096], P(None, ('row', 'col')), may hold values from -4 to 4
Outputs:
- propagated: float32 [2, 512, 4096], P(None, 'row', 'col')
All inputs are finite; a program needn't handle non-finite values.
Results may differ from a plain program's by a relative error of at most 0.0003.
Values may be sent and summed in bfloat16 or wider, within the bound.
A program may use at most 64 MiB of HBM per device.

v0:
```python
import jax
import jax.numpy as jnp
from jax import lax
from jax.sharding import PartitionSpec as P

STEPS = 2
diffraction = 0.15
phase_gain = 0.25


def with_halo(cells, sides, width):
    for axis, dim in sides:
        count = lax.axis_size(axis)
        head = lax.slice_in_dim(cells, 0, width, axis=dim)
        tail = lax.slice_in_dim(cells, cells.shape[dim] - width, cells.shape[dim], axis=dim)
        cells = jnp.concatenate(
            [
                lax.ppermute(tail, axis, [(i, (i + 1) % count) for i in range(count)]),
                cells,
                lax.ppermute(head, axis, [((i + 1) % count, i) for i in range(count)]),
            ],
            axis=dim,
        )
    return cells


def laplace(padded):
    centre = padded[:, 2:-2, 2:-2]
    along_y = 16.0 * (padded[:, 1:-3, 2:-2] + padded[:, 3:-1, 2:-2]) - (
        padded[:, :-4, 2:-2] + padded[:, 4:, 2:-2]
    )
    along_x = 16.0 * (padded[:, 2:-2, 1:-3] + padded[:, 2:-2, 3:-1]) - (
        padded[:, 2:-2, :-4] + padded[:, 2:-2, 4:]
    )
    return (along_y + along_x - 60.0 * centre) / 12.0


def slope(padded, plane):
    centre = padded[:, 2:-2, 2:-2]
    total = diffraction * laplace(padded) + phase_gain * plane.astype(jnp.float32) * centre
    return jnp.stack([-total[1], total[0]])


def section_slope(state, plane):
    padded = with_halo(state, (("row", 1), ("col", 2)), 2)
    return slope(padded, plane)


def local(optical_field, index_panels):
    planes_all = lax.all_to_all(index_panels, "col", split_axis=2, concat_axis=1, tiled=True)
    field = optical_field
    planes = None
    for step_index in range(STEPS):
        first = 2 * step_index
        planes = planes_all[first : first + 3]
        first_slope = section_slope(field, planes[0])
        second_slope = section_slope(field + 0.5 * first_slope, planes[1])
        third_slope = section_slope(field + 0.5 * second_slope, planes[1])
        fourth_slope = section_slope(field + third_slope, planes[2])
        field = field + (first_slope + 2.0 * second_slope + 2.0 * third_slope + fourth_slope) / 6.0
    return field


def solution(mesh):
    in_specs = (P(None, "row", "col"), P(None, ("row", "col"), None))
    out_specs = P(None, "row", "col")
    return jax.shard_map(local, mesh=mesh, in_specs=in_specs, out_specs=out_specs, check_vma=False)
```

profile of v0, /device:TPU:0, one launch (start us, length us, event | category | flops | bytes accessed | tf_op | source)
XLA Modules:
  0.0 162.4 jit_solution(11394870547222477419)
XLA Ops:
  0.0 8.1 %copy.10 = bf16[5,16,4096]{1,0,2:T(8,128)(2,1)} copy(bf16[5,16,4096]{2,1,0:T(8,128)(2,1)} %param.3) | data formatting | bytes 1310720 | tf_op args[1]
  8.1 9.1 %reshape.60 = bf16[8,2,20480]{2,1,0:T(2,128)(2,1)} reshape(bf16[4096,5,16]{2,1,0:T(8,128)(2,1)} %bitcast.10) | data formatting | bytes 1310720
  17.2 7.3 %all-to-all-start = ((bf16[8,2,20480]{2,1,0:T(2,128)(2,1)}), bf16[8,2,20480]{2,1,0:T(2,128)(2,1)S(1)}, u32[]{:S(2)}, u32[]{:S(2)}) async-start(bf16[8,2,20480]{2,1,0:T(2,128)(2,1)} %reshape.60), calls=%async_computation | async-start | bytes 1310720 | tf_op jit(solution)/shard_map/all_to_all | solution.py:50
  27.8 2.1 %collective-permute-start.2 = (f32[2,132,2]{2,1,0:T(8,128)S(1)}, f32[2,132,2]{2,1,0:T(8,128)S(1)}, u32[]{:S(2)}, u32[]{:S(2)}) collective-permute-start(f32[2,132,2]{2,1,0:T(8,128)S(1)} %get-tuple-element.40), channel_id=1, source_target_pairs={{0,1},{1,2},{2,3},{3,4},{4,5},{5,6},{6,7},{7,0},{8,9},{9,10},{10,1... | collective-permute-start | bytes 6344 | tf_op jit(solution)/shard_map/ppermute | solution.py:18
  29.8 2.8 %collective-permute-start.3 = (f32[2,132,2]{2,1,0:T(8,128)S(1)}, f32[2,132,2]{2,1,0:T(8,128)S(1)}, u32[]{:S(2)}, u32[]{:S(2)}) collective-permute-start(f32[2,132,2]{2,1,0:T(8,128)S(1)} %get-tuple-element.41), channel_id=1, source_target_pairs={{1,0},{2,1},{3,2},{4,3},{5,4},{6,5},{7,6},{0,7},{9,8},{10,9},{11,1... | collective-permute-start | bytes 6344 | tf_op jit(solution)/shard_map/ppermute | solution.py:20
  32.6 10.5 %collective-permute-done.2 = f32[2,132,2]{2,1,0:T(8,128)S(1)} collective-permute-done((f32[2,132,2]{2,1,0:T(8,128)S(1)}, f32[2,132,2]{2,1,0:T(8,128)S(1)}, u32[]{:S(2)}, u32[]{:S(2)}) %collective-permute-start.2) | collective-permute-done | bytes 2144 | tf_op jit(solution)/shard_map/ppermute | solution.py:18
  43.4 7.3 %reshape.61 = bf16[4096,5,16]{2,1,0:T(8,128)(2,1)} reshape(bf16[8,2,20480]{2,1,0:T(2,128)(2,1)S(1)} %all-to-all-done) | data formatting | bytes 1310720
  50.7 6.4 %copy.17 = bf16[5,16,8,512]{3,2,1,0:T(8,128)(2,1)S(1)} copy(bf16[5,16,8,512]{1,0,3,2:T(8,128)(2,1)} %bitcast.9) | data formatting | bytes 1310720 | tf_op jit(solution)/shard_map/all_to_all | solution.py:50
  61.5 2.8 %collective-permute-start.6 = (f32[2,132,2]{2,1,0:T(8,128)S(1)}, f32[2,132,2]{2,1,0:T(8,128)S(1)}, u32[]{:S(2)}, u32[]{:S(2)}) collective-permute-start(f32[2,132,2]{2,1,0:T(8,128)S(1)} %get-tuple-element.36), channel_id=1, source_target_pairs={{0,1},{1,2},{2,3},{3,4},{4,5},{5,6},{6,7},{7,0},{8,9},{9,10},{10,1... | collective-permute-start | bytes 6344 | tf_op jit(solution)/shard_map/ppermute | solution.py:18
  64.3 2.0 %collective-permute-start.7 = (f32[2,132,2]{2,1,0:T(8,128)S(1)}, f32[2,132,2]{2,1,0:T(8,128)S(1)}, u32[]{:S(2)}, u32[]{:S(2)}) collective-permute-start(f32[2,132,2]{2,1,0:T(8,128)S(1)} %get-tuple-element.37), channel_id=1, source_target_pairs={{1,0},{2,1},{3,2},{4,3},{5,4},{6,5},{7,6},{0,7},{9,8},{10,9},{11,1... | collective-permute-start | bytes 6344 | tf_op jit(solution)/shard_map/ppermute | solution.py:20
  66.5 4.4 %collective-permute-done.6 = f32[2,132,2]{2,1,0:T(8,128)S(1)} collective-permute-done((f32[2,132,2]{2,1,0:T(8,128)S(1)}, f32[2,132,2]{2,1,0:T(8,128)S(1)}, u32[]{:S(2)}, u32[]{:S(2)}) %collective-permute-start.6) | collective-permute-done | bytes 2144 | tf_op jit(solution)/shard_map/ppermute | solution.py:18
  70.8 2.9 %collective-permute-done.7 = f32[2,132,2]{2,1,0:T(8,128)S(1)} collective-permute-done((f32[2,132,2]{2,1,0:T(8,128)S(1)}, f32[2,132,2]{2,1,0:T(8,128)S(1)}, u32[]{:S(2)}, u32[]{:S(2)}) %collective-permute-start.7) | collective-permute-done | bytes 2144 | tf_op jit(solution)/shard_map/ppermute | solution.py:20
  78.2 4.7 %collective-permute-start.11 = (f32[2,132,2]{2,1,0:T(8,128)S(1)}, f32[2,132,2]{2,1,0:T(8,128)S(1)}, u32[]{:S(2)}, u32[]{:S(2)}) collective-permute-start(f32[2,132,2]{2,1,0:T(8,128)S(1)} %get-tuple-element.33), channel_id=1, source_target_pairs={{1,0},{2,1},{3,2},{4,3},{5,4},{6,5},{7,6},{0,7},{9,8},{10,9},{11,1... | collective-permute-start | bytes 6344 | tf_op jit(solution)/shard_map/ppermute | solution.py:20
  82.9 4.6 %collective-permute-done.10 = f32[2,132,2]{2,1,0:T(8,128)S(1)} collective-permute-done((f32[2,132,2]{2,1,0:T(8,128)S(1)}, f32[2,132,2]{2,1,0:T(8,128)S(1)}, u32[]{:S(2)}, u32[]{:S(2)}) %collective-permute-start.10) | collective-permute-done | bytes 2144 | tf_op jit(solution)/shard_map/ppermute | solution.py:18
  92.2 4.7 %collective-permute-start.15 = (f32[2,132,2]{2,1,0:T(8,128)S(1)}, f32[2,132,2]{2,1,0:T(8,128)S(1)}, u32[]{:S(2)}, u32[]{:S(2)}) collective-permute-start(f32[2,132,2]{2,1,0:T(8,128)S(1)} %get-tuple-element.29), channel_id=1, source_target_pairs={{1,0},{2,1},{3,2},{4,3},{5,4},{6,5},{7,6},{0,7},{9,8},{10,9},{11,1... | collective-permute-start | bytes 6344 | tf_op jit(solution)/shard_map/ppermute | solution.py:20
  97.1 4.2 %collective-permute-done.14 = f32[2,132,2]{2,1,0:T(8,128)S(1)} collective-permute-done((f32[2,132,2]{2,1,0:T(8,128)S(1)}, f32[2,132,2]{2,1,0:T(8,128)S(1)}, u32[]{:S(2)}, u32[]{:S(2)}) %collective-permute-start.14) | collective-permute-done | bytes 2144 | tf_op jit(solution)/shard_map/ppermute | solution.py:18
  105.9 5.1 %collective-permute-start.19 = (f32[2,132,2]{2,1,0:T(8,128)S(1)}, f32[2,132,2]{2,1,0:T(8,128)S(1)}, u32[]{:S(2)}, u32[]{:S(2)}) collective-permute-start(f32[2,132,2]{2,1,0:T(8,128)S(1)} %get-tuple-element.25), channel_id=1, source_target_pairs={{1,0},{2,1},{3,2},{4,3},{5,4},{6,5},{7,6},{0,7},{9,8},{10,9},{11,1... | collective-permute-start | bytes 6344 | tf_op jit(solution)/shard_map/ppermute | solution.py:20
  111.0 3.8 %collective-permute-done.18 = f32[2,132,2]{2,1,0:T(8,128)S(1)} collective-permute-done((f32[2,132,2]{2,1,0:T(8,128)S(1)}, f32[2,132,2]{2,1,0:T(8,128)S(1)}, u32[]{:S(2)}, u32[]{:S(2)}) %collective-permute-start.18) | collective-permute-done | bytes 2144 | tf_op jit(solution)/shard_map/ppermute | solution.py:18
  119.7 5.3 %collective-permute-start.23 = (f32[2,132,2]{2,1,0:T(8,128)S(1)}, f32[2,132,2]{2,1,0:T(8,128)S(1)}, u32[]{:S(2)}, u32[]{:S(2)}) collective-permute-start(f32[2,132,2]{2,1,0:T(8,128)S(1)} %get-tuple-element.21), channel_id=1, source_target_pairs={{1,0},{2,1},{3,2},{4,3},{5,4},{6,5},{7,6},{0,7},{9,8},{10,9},{11,1... | collective-permute-start | bytes 6344 | tf_op jit(solution)/shard_map/ppermute | solution.py:20
  125.1 3.9 %collective-permute-done.22 = f32[2,132,2]{2,1,0:T(8,128)S(1)} collective-permute-done((f32[2,132,2]{2,1,0:T(8,128)S(1)}, f32[2,132,2]{2,1,0:T(8,128)S(1)}, u32[]{:S(2)}, u32[]{:S(2)}) %collective-permute-start.22) | collective-permute-done | bytes 2144 | tf_op jit(solution)/shard_map/ppermute | solution.py:18
  134.7 4.5 %collective-permute-start.27 = (f32[2,132,2]{2,1,0:T(8,128)S(1)}, f32[2,132,2]{2,1,0:T(8,128)S(1)}, u32[]{:S(2)}, u32[]{:S(2)}) collective-permute-start(f32[2,132,2]{2,1,0:T(8,128)S(1)} %get-tuple-element.17), channel_id=1, source_target_pairs={{1,0},{2,1},{3,2},{4,3},{5,4},{6,5},{7,6},{0,7},{9,8},{10,9},{11,1... | collective-permute-start | bytes 6344 | tf_op jit(solution)/shard_map/ppermute | solution.py:20
  139.3 4.2 %collective-permute-done.26 = f32[2,132,2]{2,1,0:T(8,128)S(1)} collective-permute-done((f32[2,132,2]{2,1,0:T(8,128)S(1)}, f32[2,132,2]{2,1,0:T(8,128)S(1)}, u32[]{:S(2)}, u32[]{:S(2)}) %collective-permute-start.26) | collective-permute-done | bytes 2144 | tf_op jit(solution)/shard_map/ppermute | solution.py:18
  149.8 4.5 %collective-permute-start.31 = (f32[2,132,2]{2,1,0:T(8,128)S(1)}, f32[2,132,2]{2,1,0:T(8,128)S(1)}, u32[]{:S(2)}, u32[]{:S(2)}) collective-permute-start(f32[2,132,2]{2,1,0:T(8,128)S(1)} %get-tuple-element.13), channel_id=1, source_target_pairs={{1,0},{2,1},{3,2},{4,3},{5,4},{6,5},{7,6},{0,7},{9,8},{10,9},{11,1... | collective-permute-start | bytes 6344 | tf_op jit(solution)/shard_map/ppermute | solution.py:20
  154.5 4.0 %collective-permute-done.30 = f32[2,132,2]{2,1,0:T(8,128)S(1)} collective-permute-done((f32[2,132,2]{2,1,0:T(8,128)S(1)}, f32[2,132,2]{2,1,0:T(8,128)S(1)}, u32[]{:S(2)}, u32[]{:S(2)}) %collective-permute-start.30) | collective-permute-done | bytes 2144 | tf_op jit(solution)/shard_map/ppermute | solution.py:18
  (104 shorter events, 42.9 us)
Async XLA Ops:
  17.2 26.2 %all-to-all-start = ((bf16[8,2,20480]{2,1,0:T(2,128)(2,1)}), bf16[8,2,20480]{2,1,0:T(2,128)(2,1)S(1)}, u32[]{:S(2)}, u32[]{:S(2)}) async-start(bf16[8,2,20480]{2,1,0:T(2,128)(2,1)} %reshape.60), calls=%async_computation | async-start | bytes 1310720 | tf_op jit(solution)/shard_map/all_to_all | solution.py:50
  24.5 3.1 %collective-permute-start = (f32[2,2,512]{2,1,0:T(2,128)S(1)}, f32[2,2,512]{2,1,0:T(2,128)S(1)}, u32[]{:S(2)}, u32[]{:S(2)}) collective-permute-start(f32[2,2,512]{2,1,0:T(2,128)S(1)} %get-tuple-element.73), channel_id=1, source_target_pairs={{0,8},{8,16},{16,24},{24,0},{1,9},{9,17},{17,25},{25,1},{2,10},{10... | collective-permute-start | bytes 24584 | tf_op jit(solution)/shard_map/ppermute | solution.py:18
  27.8 15.4 %collective-permute-start.2 = (f32[2,132,2]{2,1,0:T(8,128)S(1)}, f32[2,132,2]{2,1,0:T(8,128)S(1)}, u32[]{:S(2)}, u32[]{:S(2)}) collective-permute-start(f32[2,132,2]{2,1,0:T(8,128)S(1)} %get-tuple-element.40), channel_id=1, source_target_pairs={{0,1},{1,2},{2,3},{3,4},{4,5},{5,6},{6,7},{7,0},{8,9},{9,10},{10,1... | collective-permute-start | bytes 6344 | tf_op jit(solution)/shard_map/ppermute | solution.py:18
  29.8 13.3 %collective-permute-start.3 = (f32[2,132,2]{2,1,0:T(8,128)S(1)}, f32[2,132,2]{2,1,0:T(8,128)S(1)}, u32[]{:S(2)}, u32[]{:S(2)}) collective-permute-start(f32[2,132,2]{2,1,0:T(8,128)S(1)} %get-tuple-element.41), channel_id=1, source_target_pairs={{1,0},{2,1},{3,2},{4,3},{5,4},{6,5},{7,6},{0,7},{9,8},{10,9},{11,1... | collective-permute-start | bytes 6344 | tf_op jit(solution)/shard_map/ppermute | solution.py:20
  58.2 3.1 %collective-permute-start.4 = (f32[2,2,512]{2,1,0:T(2,128)S(1)}, f32[2,2,512]{2,1,0:T(2,128)S(1)}, u32[]{:S(2)}, u32[]{:S(2)}) collective-permute-start(f32[2,2,512]{2,1,0:T(2,128)S(1)} %get-tuple-element.68), channel_id=1, source_target_pairs={{0,8},{8,16},{16,24},{24,0},{1,9},{9,17},{17,25},{25,1},{2,10},{10... | collective-permute-start | bytes 24584 | tf_op jit(solution)/shard_map/ppermute | solution.py:18
  61.5 9.3 %collective-permute-start.6 = (f32[2,132,2]{2,1,0:T(8,128)S(1)}, f32[2,132,2]{2,1,0:T(8,128)S(1)}, u32[]{:S(2)}, u32[]{:S(2)}) collective-permute-start(f32[2,132,2]{2,1,0:T(8,128)S(1)} %get-tuple-element.36), channel_id=1, source_target_pairs={{0,1},{1,2},{2,3},{3,4},{4,5},{5,6},{6,7},{7,0},{8,9},{9,10},{10,1... | collective-permute-start | bytes 6344 | tf_op jit(solution)/shard_map/ppermute | solution.py:18
  64.3 9.4 %collective-permute-start.7 = (f32[2,132,2]{2,1,0:T(8,128)S(1)}, f32[2,132,2]{2,1,0:T(8,128)S(1)}, u32[]{:S(2)}, u32[]{:S(2)}) collective-permute-start(f32[2,132,2]{2,1,0:T(8,128)S(1)} %get-tuple-element.37), channel_id=1, source_target_pairs={{1,0},{2,1},{3,2},{4,3},{5,4},{6,5},{7,6},{0,7},{9,8},{10,9},{11,1... | collective-permute-start | bytes 6344 | tf_op jit(solution)/shard_map/ppermute | solution.py:20
  74.9 3.1 %collective-permute-start.8 = (f32[2,2,512]{2,1,0:T(2,128)S(1)}, f32[2,2,512]{2,1,0:T(2,128)S(1)}, u32[]{:S(2)}, u32[]{:S(2)}) collective-permute-start(f32[2,2,512]{2,1,0:T(2,128)S(1)} %get-tuple-element.64), channel_id=1, source_target_pairs={{0,8},{8,16},{16,24},{24,0},{1,9},{9,17},{17,25},{25,1},{2,10},{10... | collective-permute-start | bytes 24584 | tf_op jit(solution)/shard_map/ppermute | solution.py:18
  78.2 9.3 %collective-permute-start.10 = (f32[2,132,2]{2,1,0:T(8,128)S(1)}, f32[2,132,2]{2,1,0:T(8,128)S(1)}, u32[]{:S(2)}, u32[]{:S(2)}) collective-permute-start(f32[2,132,2]{2,1,0:T(8,128)S(1)} %get-tuple-element.32), channel_id=1, source_target_pairs={{0,1},{1,2},{2,3},{3,4},{4,5},{5,6},{6,7},{7,0},{8,9},{9,10},{10,1... | collective-permute-start | bytes 6344 | tf_op jit(solution)/shard_map/ppermute | solution.py:18
  78.2 9.5 %collective-permute-start.11 = (f32[2,132,2]{2,1,0:T(8,128)S(1)}, f32[2,132,2]{2,1,0:T(8,128)S(1)}, u32[]{:S(2)}, u32[]{:S(2)}) collective-permute-start(f32[2,132,2]{2,1,0:T(8,128)S(1)} %get-tuple-element.33), channel_id=1, source_target_pairs={{1,0},{2,1},{3,2},{4,3},{5,4},{6,5},{7,6},{0,7},{9,8},{10,9},{11,1... | collective-permute-start | bytes 6344 | tf_op jit(solution)/shard_map/ppermute | solution.py:20
  88.8 3.1 %collective-permute-start.12 = (f32[2,2,512]{2,1,0:T(2,128)S(1)}, f32[2,2,512]{2,1,0:T(2,128)S(1)}, u32[]{:S(2)}, u32[]{:S(2)}) collective-permute-start(f32[2,2,512]{2,1,0:T(2,128)S(1)} %get-tuple-element.60), channel_id=1, source_target_pairs={{0,8},{8,16},{16,24},{24,0},{1,9},{9,17},{17,25},{25,1},{2,10},{10... | collective-permute-start | bytes 24584 | tf_op jit(solution)/shard_map/ppermute | solution.py:18
  92.1 9.1 %collective-permute-start.14 = (f32[2,132,2]{2,1,0:T(8,128)S(1)}, f32[2,132,2]{2,1,0:T(8,128)S(1)}, u32[]{:S(2)}, u32[]{:S(2)}) collective-permute-start(f32[2,132,2]{2,1,0:T(8,128)S(1)} %get-tuple-element.28), channel_id=1, source_target_pairs={{0,1},{1,2},{2,3},{3,4},{4,5},{5,6},{6,7},{7,0},{8,9},{9,10},{10,1... | collective-permute-start | bytes 6344 | tf_op jit(solution)/shard_map/ppermute | solution.py:18
  92.2 9.0 %collective-permute-start.15 = (f32[2,132,2]{2,1,0:T(8,128)S(1)}, f32[2,132,2]{2,1,0:T(8,128)S(1)}, u32[]{:S(2)}, u32[]{:S(2)}) collective-permute-start(f32[2,132,2]{2,1,0:T(8,128)S(1)} %get-tuple-element.29), channel_id=1, source_target_pairs={{1,0},{2,1},{3,2},{4,3},{5,4},{6,5},{7,6},{0,7},{9,8},{10,9},{11,1... | collective-permute-start | bytes 6344 | tf_op jit(solution)/shard_map/ppermute | solution.py:20
  102.5 3.1 %collective-permute-start.16 = (f32[2,2,512]{2,1,0:T(2,128)S(1)}, f32[2,2,512]{2,1,0:T(2,128)S(1)}, u32[]{:S(2)}, u32[]{:S(2)}) collective-permute-start(f32[2,2,512]{2,1,0:T(2,128)S(1)} %get-tuple-element.56), channel_id=1, source_target_pairs={{0,8},{8,16},{16,24},{24,0},{1,9},{9,17},{17,25},{25,1},{2,10},{10... | collective-permute-start | bytes 24584 | tf_op jit(solution)/shard_map/ppermute | solution.py:18
  105.8 9.0 %collective-permute-start.18 = (f32[2,132,2]{2,1,0:T(8,128)S(1)}, f32[2,132,2]{2,1,0:T(8,128)S(1)}, u32[]{:S(2)}, u32[]{:S(2)}) collective-permute-start(f32[2,132,2]{2,1,0:T(8,128)S(1)} %get-tuple-element.24), channel_id=1, source_target_pairs={{0,1},{1,2},{2,3},{3,4},{4,5},{5,6},{6,7},{7,0},{8,9},{9,10},{10,1... | collective-permute-start | bytes 6344 | tf_op jit(solution)/shard_map/ppermute | solution.py:18
  105.9 9.1 %collective-permute-start.19 = (f32[2,132,2]{2,1,0:T(8,128)S(1)}, f32[2,132,2]{2,1,0:T(8,128)S(1)}, u32[]{:S(2)}, u32[]{:S(2)}) collective-permute-start(f32[2,132,2]{2,1,0:T(8,128)S(1)} %get-tuple-element.25), channel_id=1, source_target_pairs={{1,0},{2,1},{3,2},{4,3},{5,4},{6,5},{7,6},{0,7},{9,8},{10,9},{11,1... | collective-permute-start | bytes 6344 | tf_op jit(solution)/shard_map/ppermute | solution.py:20
  116.3 3.1 %collective-permute-start.20 = (f32[2,2,512]{2,1,0:T(2,128)S(1)}, f32[2,2,512]{2,1,0:T(2,128)S(1)}, u32[]{:S(2)}, u32[]{:S(2)}) collective-permute-start(f32[2,2,512]{2,1,0:T(2,128)S(1)} %get-tuple-element.52), channel_id=1, source_target_pairs={{0,8},{8,16},{16,24},{24,0},{1,9},{9,17},{17,25},{25,1},{2,10},{10... | collective-permute-start | bytes 24584 | tf_op jit(solution)/shard_map/ppermute | solution.py:18
  119.6 9.4 %collective-permute-start.22 = (f32[2,132,2]{2,1,0:T(8,128)S(1)}, f32[2,132,2]{2,1,0:T(8,128)S(1)}, u32[]{:S(2)}, u32[]{:S(2)}) collective-permute-start(f32[2,132,2]{2,1,0:T(8,128)S(1)} %get-tuple-element.20), channel_id=1, source_target_pairs={{0,1},{1,2},{2,3},{3,4},{4,5},{5,6},{6,7},{7,0},{8,9},{9,10},{10,1... | collective-permute-start | bytes 6344 | tf_op jit(solution)/shard_map/ppermute | solution.py:18
  119.7 10.2 %collective-permute-start.23 = (f32[2,132,2]{2,1,0:T(8,128)S(1)}, f32[2,132,2]{2,1,0:T(8,128)S(1)}, u32[]{:S(2)}, u32[]{:S(2)}) collective-permute-start(f32[2,132,2]{2,1,0:T(8,128)S(1)} %get-tuple-element.21), channel_id=1, source_target_pairs={{1,0},{2,1},{3,2},{4,3},{5,4},{6,5},{7,6},{0,7},{9,8},{10,9},{11,1... | collective-permute-start | bytes 6344 | tf_op jit(solution)/shard_map/ppermute | solution.py:20
  131.2 3.1 %collective-permute-start.24 = (f32[2,2,512]{2,1,0:T(2,128)S(1)}, f32[2,2,512]{2,1,0:T(2,128)S(1)}, u32[]{:S(2)}, u32[]{:S(2)}) collective-permute-start(f32[2,2,512]{2,1,0:T(2,128)S(1)} %get-tuple-element.48), channel_id=1, source_target_pairs={{0,8},{8,16},{16,24},{24,0},{1,9},{9,17},{17,25},{25,1},{2,10},{10... | collective-permute-start | bytes 24584 | tf_op jit(solution)/shard_map/ppermute | solution.py:18
  134.5 9.0 %collective-permute-start.26 = (f32[2,132,2]{2,1,0:T(8,128)S(1)}, f32[2,132,2]{2,1,0:T(8,128)S(1)}, u32[]{:S(2)}, u32[]{:S(2)}) collective-permute-start(f32[2,132,2]{2,1,0:T(8,128)S(1)} %get-tuple-element.16), channel_id=1, source_target_pairs={{0,1},{1,2},{2,3},{3,4},{4,5},{5,6},{6,7},{7,0},{8,9},{9,10},{10,1... | collective-permute-start | bytes 6344 | tf_op jit(solution)/shard_map/ppermute | solution.py:18
  134.7 10.2 %collective-permute-start.27 = (f32[2,132,2]{2,1,0:T(8,128)S(1)}, f32[2,132,2]{2,1,0:T(8,128)S(1)}, u32[]{:S(2)}, u32[]{:S(2)}) collective-permute-start(f32[2,132,2]{2,1,0:T(8,128)S(1)} %get-tuple-element.17), channel_id=1, source_target_pairs={{1,0},{2,1},{3,2},{4,3},{5,4},{6,5},{7,6},{0,7},{9,8},{10,9},{11,1... | collective-permute-start | bytes 6344 | tf_op jit(solution)/shard_map/ppermute | solution.py:20
  149.6 9.0 %collective-permute-start.30 = (f32[2,132,2]{2,1,0:T(8,128)S(1)}, f32[2,132,2]{2,1,0:T(8,128)S(1)}, u32[]{:S(2)}, u32[]{:S(2)}) collective-permute-start(f32[2,132,2]{2,1,0:T(8,128)S(1)} %get-tuple-element.12), channel_id=1, source_target_pairs={{0,1},{1,2},{2,3},{3,4},{4,5},{5,6},{6,7},{7,0},{8,9},{9,10},{10,1... | collective-permute-start | bytes 6344 | tf_op jit(solution)/shard_map/ppermute | solution.py:18
  149.8 10.2 %collective-permute-start.31 = (f32[2,132,2]{2,1,0:T(8,128)S(1)}, f32[2,132,2]{2,1,0:T(8,128)S(1)}, u32[]{:S(2)}, u32[]{:S(2)}) collective-permute-start(f32[2,132,2]{2,1,0:T(8,128)S(1)} %get-tuple-element.13), channel_id=1, source_target_pairs={{1,0},{2,1},{3,2},{4,3},{5,4},{6,5},{7,6},{0,7},{9,8},{10,9},{11,1... | collective-permute-start | bytes 6344 | tf_op jit(solution)/shard_map/ppermute | solution.py:20
  (10 other events, 51.2 us)
where the time goes:
time: 163 us; the launch traced here: 162 us
  starting transfers between devices  60.8 us (37%)
  waiting for transfers between devices  57.7 us (35%)
  local copies, waits for them, and re-layouts  31.8 us (20%)
  other arithmetic  11.7 us (7%)
    ppermute x16, waiting for transfers between devices, with_halo(): lax.ppermute(tail, axis, [(i, (i + 1) % count) for i in range(count)])  50.1 us
    ppermute x16, starting transfers between devices, with_halo(): lax.ppermute(head, axis, [((i + 1) % count, i) for i in range(count)])  46.3 us
    unnamed x6, local copies, waits for them, and re-layouts  24.5 us
    ppermute x16, waiting for transfers between devices, with_halo(): lax.ppermute(head, axis, [((i + 1) % count, i) for i in range(count)])  7.54 us
    ppermute x16, starting transfers between devices, with_halo(): lax.ppermute(tail, axis, [(i, (i + 1) % count) for i in range(count)])  7.29 us
    all_to_all x1, starting transfers between devices, local(): lax.all_to_all(index_panels, 'col', split_axis=2, concat_axis=1, tiled=True)  7.28 us
    all_to_all x1, local copies, waits for them, and re-layouts, local(): lax.all_to_all(index_panels, 'col', split_axis=2, concat_axis=1, tiled=True)  6.41 us
    add x8, other arithmetic, slope(): diffraction * laplace(padded)  4.96 us
  transfers between devices with their start and end apart: 33, of which 22 were waited for; matrix products, arithmetic and copies ran while one was open for 1% of the time, Pallas kernels for 0%

commit v1 on v0

--- a/solution.py
+++ b/solution.py
@@ -47,7 +47,12 @@
 
 
 def local(optical_field, index_panels):
-    planes_all = lax.all_to_all(index_panels, "col", split_axis=2, concat_axis=1, tiled=True)
+    planes_all = jnp.concatenate(
+        lax.all_to_all(
+            jnp.stack(jnp.split(index_panels, lax.axis_size("col"), axis=2)), "col", 0, 0
+        ),
+        axis=1,
+    )
     field = optical_field
     planes = None
     for step_index in range(STEPS):

time: 163 us -> 144 us (0.88)
  local copies, waits for them, and re-layouts: 31.8 us -> 12.3 us
    unnamed x6 -> x10, local copies, waits for them, and re-layouts: 24.5 us -> 10.7 us
    all_to_all x1 -> x0, local copies, waits for them, and re-layouts: 6.41 us -> none  [local(): lax.all_to_all(index_panels, 'col', split_axis=2, concat_axis=1, tiled=True)]
  transfers between devices with their start and end apart: 33 -> 33, of which waited for: 22 -> 22; matrix products, arithmetic and copies ran while one was open for 1% -> 0% of each run, Pallas kernels for 0% -> 0%
where the time goes in v1:
time: 144 us
  starting transfers between devices  60.1 us (42%)
  waiting for transfers between devices  59 us (41%)
  local copies, waits for them, and re-layouts  12.3 us (9%)
  other arithmetic  11.7 us (8%)
    ppermute x16, waiting for transfers between devices, with_halo(): lax.ppermute(tail, axis, [(i, (i + 1) % count) for i in range(count)])  50.8 us
    ppermute x16, starting transfers between devices, with_halo(): lax.ppermute(head, axis, [((i + 1) % count, i) for i in range(count)])  45.8 us
    unnamed x10, local copies, waits for them, and re-layouts  10.7 us
    ppermute x16, waiting for transfers between devices, with_halo(): lax.ppermute(head, axis, [((i + 1) % count, i) for i in range(count)])  8.25 us
    all_to_all x1, starting transfers between devices, local(): lax.all_to_all(jnp.stack(jnp.split(index_panels, lax.axis_size('col'), ax...  7.41 us
    ppermute x16, starting transfers between devices, with_halo(): lax.ppermute(tail, axis, [(i, (i + 1) % count) for i in range(count)])  6.97 us
    add x8, other arithmetic, slope(): diffraction * laplace(padded)  4.96 us
  transfers between devices with their start and end apart: 33, of which 22 were waited for; matrix products, arithmetic and copies ran while one was open for 0% of the time, Pallas kernels for 0%

profile of v1, /device:TPU:0, one launch (start us, length us, event | category | flops | bytes accessed | tf_op | source)
XLA Modules:
  0.0 143.6 jit_solution(13973525090332238260)
XLA Ops:
  12.2 7.4 %all-to-all-start = ((bf16[8,5,16,512]{3,2,1,0:T(8,128)(2,1)}), bf16[8,5,16,512]{3,2,1,0:T(8,128)(2,1)S(1)}, u32[]{:S(2)}, u32[]{:S(2)}) async-start(bf16[8,5,16,512]{3,2,1,0:T(8,128)(2,1)} %bitcast_dynamic-update-slice_fusion), calls=%async_computation | async-start | bytes 1310720 | tf_op jit(solution)/shard_map/all_to_all | solution.py:51
  21.7 1.7 %collective-permute-done = f32[2,2,512]{2,1,0:T(2,128)S(1)} collective-permute-done((f32[2,2,512]{2,1,0:T(2,128)S(1)}, f32[2,2,512]{2,1,0:T(2,128)S(1)}, u32[]{:S(2)}, u32[]{:S(2)}) %collective-permute-start) | collective-permute-done | bytes 8224 | tf_op jit(solution)/shard_map/ppermute | solution.py:18
  23.5 1.8 %collective-permute-start.2 = (f32[2,132,2]{2,1,0:T(8,128)S(1)}, f32[2,132,2]{2,1,0:T(8,128)S(1)}, u32[]{:S(2)}, u32[]{:S(2)}) collective-permute-start(f32[2,132,2]{2,1,0:T(8,128)S(1)} %get-tuple-element.40), channel_id=1, source_target_pairs={{0,1},{1,2},{2,3},{3,4},{4,5},{5,6},{6,7},{7,0},{8,9},{9,10},{10,1... | collective-permute-start | bytes 6344 | tf_op jit(solution)/shard_map/ppermute | solution.py:18
  25.3 3.0 %collective-permute-start.3 = (f32[2,132,2]{2,1,0:T(8,128)S(1)}, f32[2,132,2]{2,1,0:T(8,128)S(1)}, u32[]{:S(2)}, u32[]{:S(2)}) collective-permute-start(f32[2,132,2]{2,1,0:T(8,128)S(1)} %get-tuple-element.41), channel_id=1, source_target_pairs={{1,0},{2,1},{3,2},{4,3},{5,4},{6,5},{7,6},{0,7},{9,8},{10,9},{11,1... | collective-permute-start | bytes 6344 | tf_op jit(solution)/shard_map/ppermute | solution.py:20
  28.3 10.0 %collective-permute-done.2 = f32[2,132,2]{2,1,0:T(8,128)S(1)} collective-permute-done((f32[2,132,2]{2,1,0:T(8,128)S(1)}, f32[2,132,2]{2,1,0:T(8,128)S(1)}, u32[]{:S(2)}, u32[]{:S(2)}) %collective-permute-start.2) | collective-permute-done | bytes 2144 | tf_op jit(solution)/shard_map/ppermute | solution.py:18
  39.6 1.7 %collective-permute-start.5 = (f32[2,2,512]{2,1,0:T(2,128)S(1)}, f32[2,2,512]{2,1,0:T(2,128)S(1)}, u32[]{:S(2)}, u32[]{:S(2)}) collective-permute-start(f32[2,2,512]{2,1,0:T(2,128)S(1)} %get-tuple-element.69), channel_id=1, source_target_pairs={{8,0},{16,8},{24,16},{0,24},{9,1},{17,9},{25,17},{1,25},{10,2},{18... | collective-permute-start | bytes 24584 | tf_op jit(solution)/shard_map/ppermute | solution.py:20
  42.8 2.8 %collective-permute-start.6 = (f32[2,132,2]{2,1,0:T(8,128)S(1)}, f32[2,132,2]{2,1,0:T(8,128)S(1)}, u32[]{:S(2)}, u32[]{:S(2)}) collective-permute-start(f32[2,132,2]{2,1,0:T(8,128)S(1)} %get-tuple-element.36), channel_id=1, source_target_pairs={{0,1},{1,2},{2,3},{3,4},{4,5},{5,6},{6,7},{7,0},{8,9},{9,10},{10,1... | collective-permute-start | bytes 6344 | tf_op jit(solution)/shard_map/ppermute | solution.py:18
  45.6 2.0 %collective-permute-start.7 = (f32[2,132,2]{2,1,0:T(8,128)S(1)}, f32[2,132,2]{2,1,0:T(8,128)S(1)}, u32[]{:S(2)}, u32[]{:S(2)}) collective-permute-start(f32[2,132,2]{2,1,0:T(8,128)S(1)} %get-tuple-element.37), channel_id=1, source_target_pairs={{1,0},{2,1},{3,2},{4,3},{5,4},{6,5},{7,6},{0,7},{9,8},{10,9},{11,1... | collective-permute-start | bytes 6344 | tf_op jit(solution)/shard_map/ppermute | solution.py:20
  47.6 4.6 %collective-permute-done.6 = f32[2,132,2]{2,1,0:T(8,128)S(1)} collective-permute-done((f32[2,132,2]{2,1,0:T(8,128)S(1)}, f32[2,132,2]{2,1,0:T(8,128)S(1)}, u32[]{:S(2)}, u32[]{:S(2)}) %collective-permute-start.6) | collective-permute-done | bytes 2144 | tf_op jit(solution)/shard_map/ppermute | solution.py:18
  52.1 2.9 %collective-permute-done.7 = f32[2,132,2]{2,1,0:T(8,128)S(1)} collective-permute-done((f32[2,132,2]{2,1,0:T(8,128)S(1)}, f32[2,132,2]{2,1,0:T(8,128)S(1)}, u32[]{:S(2)}, u32[]{:S(2)}) %collective-permute-start.7) | collective-permute-done | bytes 2144 | tf_op jit(solution)/shard_map/ppermute | solution.py:20
  56.3 1.6 %collective-permute-start.9 = (f32[2,2,512]{2,1,0:T(2,128)S(1)}, f32[2,2,512]{2,1,0:T(2,128)S(1)}, u32[]{:S(2)}, u32[]{:S(2)}) collective-permute-start(f32[2,2,512]{2,1,0:T(2,128)S(1)} %get-tuple-element.65), channel_id=1, source_target_pairs={{8,0},{16,8},{24,16},{0,24},{9,1},{17,9},{25,17},{1,25},{10,2},{18... | collective-permute-start | bytes 24584 | tf_op jit(solution)/shard_map/ppermute | solution.py:20
  59.5 4.7 %collective-permute-start.11 = (f32[2,132,2]{2,1,0:T(8,128)S(1)}, f32[2,132,2]{2,1,0:T(8,128)S(1)}, u32[]{:S(2)}, u32[]{:S(2)}) collective-permute-start(f32[2,132,2]{2,1,0:T(8,128)S(1)} %get-tuple-element.33), channel_id=1, source_target_pairs={{1,0},{2,1},{3,2},{4,3},{5,4},{6,5},{7,6},{0,7},{9,8},{10,9},{11,1... | collective-permute-start | bytes 6344 | tf_op jit(solution)/shard_map/ppermute | solution.py:20
  64.2 4.6 %collective-permute-done.10 = f32[2,132,2]{2,1,0:T(8,128)S(1)} collective-permute-done((f32[2,132,2]{2,1,0:T(8,128)S(1)}, f32[2,132,2]{2,1,0:T(8,128)S(1)}, u32[]{:S(2)}, u32[]{:S(2)}) %collective-permute-start.10) | collective-permute-done | bytes 2144 | tf_op jit(solution)/shard_map/ppermute | solution.py:18
  73.4 4.7 %collective-permute-start.15 = (f32[2,132,2]{2,1,0:T(8,128)S(1)}, f32[2,132,2]{2,1,0:T(8,128)S(1)}, u32[]{:S(2)}, u32[]{:S(2)}) collective-permute-start(f32[2,132,2]{2,1,0:T(8,128)S(1)} %get-tuple-element.29), channel_id=1, source_target_pairs={{1,0},{2,1},{3,2},{4,3},{5,4},{6,5},{7,6},{0,7},{9,8},{10,9},{11,1... | collective-permute-start | bytes 6344 | tf_op jit(solution)/shard_map/ppermute | solution.py:20
  78.2 4.3 %collective-permute-done.14 = f32[2,132,2]{2,1,0:T(8,128)S(1)} collective-permute-done((f32[2,132,2]{2,1,0:T(8,128)S(1)}, f32[2,132,2]{2,1,0:T(8,128)S(1)}, u32[]{:S(2)}, u32[]{:S(2)}) %collective-permute-start.14) | collective-permute-done | bytes 2144 | tf_op jit(solution)/shard_map/ppermute | solution.py:18
  87.1 5.0 %collective-permute-start.19 = (f32[2,132,2]{2,1,0:T(8,128)S(1)}, f32[2,132,2]{2,1,0:T(8,128)S(1)}, u32[]{:S(2)}, u32[]{:S(2)}) collective-permute-start(f32[2,132,2]{2,1,0:T(8,128)S(1)} %get-tuple-element.25), channel_id=1, source_target_pairs={{1,0},{2,1},{3,2},{4,3},{5,4},{6,5},{7,6},{0,7},{9,8},{10,9},{11,1... | collective-permute-start | bytes 6344 | tf_op jit(solution)/shard_map/ppermute | solution.py:20
  92.1 4.0 %collective-permute-done.18 = f32[2,132,2]{2,1,0:T(8,128)S(1)} collective-permute-done((f32[2,132,2]{2,1,0:T(8,128)S(1)}, f32[2,132,2]{2,1,0:T(8,128)S(1)}, u32[]{:S(2)}, u32[]{:S(2)}) %collective-permute-start.18) | collective-permute-done | bytes 2144 | tf_op jit(solution)/shard_map/ppermute | solution.py:18
  100.8 5.5 %collective-permute-start.23 = (f32[2,132,2]{2,1,0:T(8,128)S(1)}, f32[2,132,2]{2,1,0:T(8,128)S(1)}, u32[]{:S(2)}, u32[]{:S(2)}) collective-permute-start(f32[2,132,2]{2,1,0:T(8,128)S(1)} %get-tuple-element.21), channel_id=1, source_target_pairs={{1,0},{2,1},{3,2},{4,3},{5,4},{6,5},{7,6},{0,7},{9,8},{10,9},{11,1... | collective-permute-start | bytes 6344 | tf_op jit(solution)/shard_map/ppermute | solution.py:20
  106.3 4.3 %collective-permute-done.22 = f32[2,132,2]{2,1,0:T(8,128)S(1)} collective-permute-done((f32[2,132,2]{2,1,0:T(8,128)S(1)}, f32[2,132,2]{2,1,0:T(8,128)S(1)}, u32[]{:S(2)}, u32[]{:S(2)}) %collective-permute-start.22) | collective-permute-done | bytes 2144 | tf_op jit(solution)/shard_map/ppermute | solution.py:18
  112.6 1.6 %collective-permute-start.25 = (f32[2,2,512]{2,1,0:T(2,128)S(1)}, f32[2,2,512]{2,1,0:T(2,128)S(1)}, u32[]{:S(2)}, u32[]{:S(2)}) collective-permute-start(f32[2,2,512]{2,1,0:T(2,128)S(1)} %get-tuple-element.49), channel_id=1, source_target_pairs={{8,0},{16,8},{24,16},{0,24},{9,1},{17,9},{25,17},{1,25},{10,2},{18... | collective-permute-start | bytes 24584 | tf_op jit(solution)/shard_map/ppermute | solution.py:20
  115.9 4.8 %collective-permute-start.27 = (f32[2,132,2]{2,1,0:T(8,128)S(1)}, f32[2,132,2]{2,1,0:T(8,128)S(1)}, u32[]{:S(2)}, u32[]{:S(2)}) collective-permute-start(f32[2,132,2]{2,1,0:T(8,128)S(1)} %get-tuple-element.17), channel_id=1, source_target_pairs={{1,0},{2,1},{3,2},{4,3},{5,4},{6,5},{7,6},{0,7},{9,8},{10,9},{11,1... | collective-permute-start | bytes 6344 | tf_op jit(solution)/shard_map/ppermute | solution.py:20
  120.7 4.0 %collective-permute-done.26 = f32[2,132,2]{2,1,0:T(8,128)S(1)} collective-permute-done((f32[2,132,2]{2,1,0:T(8,128)S(1)}, f32[2,132,2]{2,1,0:T(8,128)S(1)}, u32[]{:S(2)}, u32[]{:S(2)}) %collective-permute-start.26) | collective-permute-done | bytes 2144 | tf_op jit(solution)/shard_map/ppermute | solution.py:18
  131.0 4.5 %collective-permute-start.31 = (f32[2,132,2]{2,1,0:T(8,128)S(1)}, f32[2,132,2]{2,1,0:T(8,128)S(1)}, u32[]{:S(2)}, u32[]{:S(2)}) collective-permute-start(f32[2,132,2]{2,1,0:T(8,128)S(1)} %get-tuple-element.13), channel_id=1, source_target_pairs={{1,0},{2,1},{3,2},{4,3},{5,4},{6,5},{7,6},{0,7},{9,8},{10,9},{11,1... | collective-permute-start | bytes 6344 | tf_op jit(solution)/shard_map/ppermute | solution.py:20
  135.6 4.2 %collective-permute-done.30 = f32[2,132,2]{2,1,0:T(8,128)S(1)} collective-permute-done((f32[2,132,2]{2,1,0:T(8,128)S(1)}, f32[2,132,2]{2,1,0:T(8,128)S(1)}, u32[]{:S(2)}, u32[]{:S(2)}) %collective-permute-start.30) | collective-permute-done | bytes 2144 | tf_op jit(solution)/shard_map/ppermute | solution.py:18
  (103 shorter events, 47.6 us)
Async XLA Ops:
  12.2 26.4 %all-to-all-start = ((bf16[8,5,16,512]{3,2,1,0:T(8,128)(2,1)}), bf16[8,5,16,512]{3,2,1,0:T(8,128)(2,1)S(1)}, u32[]{:S(2)}, u32[]{:S(2)}) async-start(bf16[8,5,16,512]{3,2,1,0:T(8,128)(2,1)} %bitcast_dynamic-update-slice_fusion), calls=%async_computation | async-start | bytes 1310720 | tf_op jit(solution)/shard_map/all_to_all | solution.py:51
  23.5 14.7 %collective-permute-start.2 = (f32[2,132,2]{2,1,0:T(8,128)S(1)}, f32[2,132,2]{2,1,0:T(8,128)S(1)}, u32[]{:S(2)}, u32[]{:S(2)}) collective-permute-start(f32[2,132,2]{2,1,0:T(8,128)S(1)} %get-tuple-element.40), channel_id=1, source_target_pairs={{0,1},{1,2},{2,3},{3,4},{4,5},{5,6},{6,7},{7,0},{8,9},{9,10},{10,1... | collective-permute-start | bytes 6344 | tf_op jit(solution)/shard_map/ppermute | solution.py:18
  25.3 13.0 %collective-permute-start.3 = (f32[2,132,2]{2,1,0:T(8,128)S(1)}, f32[2,132,2]{2,1,0:T(8,128)S(1)}, u32[]{:S(2)}, u32[]{:S(2)}) collective-permute-start(f32[2,132,2]{2,1,0:T(8,128)S(1)} %get-tuple-element.41), channel_id=1, source_target_pairs={{1,0},{2,1},{3,2},{4,3},{5,4},{6,5},{7,6},{0,7},{9,8},{10,9},{11,1... | collective-permute-start | bytes 6344 | tf_op jit(solution)/shard_map/ppermute | solution.py:20
  39.5 3.1 %collective-permute-start.4 = (f32[2,2,512]{2,1,0:T(2,128)S(1)}, f32[2,2,512]{2,1,0:T(2,128)S(1)}, u32[]{:S(2)}, u32[]{:S(2)}) collective-permute-start(f32[2,2,512]{2,1,0:T(2,128)S(1)} %get-tuple-element.68), channel_id=1, source_target_pairs={{0,8},{8,16},{16,24},{24,0},{1,9},{9,17},{17,25},{25,1},{2,10},{10... | collective-permute-start | bytes 24584 | tf_op jit(solution)/shard_map/ppermute | solution.py:18
  42.8 9.3 %collective-permute-start.6 = (f32[2,132,2]{2,1,0:T(8,128)S(1)}, f32[2,132,2]{2,1,0:T(8,128)S(1)}, u32[]{:S(2)}, u32[]{:S(2)}) collective-permute-start(f32[2,132,2]{2,1,0:T(8,128)S(1)} %get-tuple-element.36), channel_id=1, source_target_pairs={{0,1},{1,2},{2,3},{3,4},{4,5},{5,6},{6,7},{7,0},{8,9},{9,10},{10,1... | collective-permute-start | bytes 6344 | tf_op jit(solution)/shard_map/ppermute | solution.py:18
  45.6 9.4 %collective-permute-start.7 = (f32[2,132,2]{2,1,0:T(8,128)S(1)}, f32[2,132,2]{2,1,0:T(8,128)S(1)}, u32[]{:S(2)}, u32[]{:S(2)}) collective-permute-start(f32[2,132,2]{2,1,0:T(8,128)S(1)} %get-tuple-element.37), channel_id=1, source_target_pairs={{1,0},{2,1},{3,2},{4,3},{5,4},{6,5},{7,6},{0,7},{9,8},{10,9},{11,1... | collective-permute-start | bytes 6344 | tf_op jit(solution)/shard_map/ppermute | solution.py:20
  56.1 3.1 %collective-permute-start.8 = (f32[2,2,512]{2,1,0:T(2,128)S(1)}, f32[2,2,512]{2,1,0:T(2,128)S(1)}, u32[]{:S(2)}, u32[]{:S(2)}) collective-permute-start(f32[2,2,512]{2,1,0:T(2,128)S(1)} %get-tuple-element.64), channel_id=1, source_target_pairs={{0,8},{8,16},{16,24},{24,0},{1,9},{9,17},{17,25},{25,1},{2,10},{10... | collective-permute-start | bytes 24584 | tf_op jit(solution)/shard_map/ppermute | solution.py:18
  59.4 9.3 %collective-permute-start.10 = (f32[2,132,2]{2,1,0:T(8,128)S(1)}, f32[2,132,2]{2,1,0:T(8,128)S(1)}, u32[]{:S(2)}, u32[]{:S(2)}) collective-permute-start(f32[2,132,2]{2,1,0:T(8,128)S(1)} %get-tuple-element.32), channel_id=1, source_target_pairs={{0,1},{1,2},{2,3},{3,4},{4,5},{5,6},{6,7},{7,0},{8,9},{9,10},{10,1... | collective-permute-start | bytes 6344 | tf_op jit(solution)/shard_map/ppermute | solution.py:18
  59.5 9.5 %collective-permute-start.11 = (f32[2,132,2]{2,1,0:T(8,128)S(1)}, f32[2,132,2]{2,1,0:T(8,128)S(1)}, u32[]{:S(2)}, u32[]{:S(2)}) collective-permute-start(f32[2,132,2]{2,1,0:T(8,128)S(1)} %get-tuple-element.33), channel_id=1, source_target_pairs={{1,0},{2,1},{3,2},{4,3},{5,4},{6,5},{7,6},{0,7},{9,8},{10,9},{11,1... | collective-permute-start | bytes 6344 | tf_op jit(solution)/shard_map/ppermute | solution.py:20
  70.1 3.1 %collective-permute-start.12 = (f32[2,2,512]{2,1,0:T(2,128)S(1)}, f32[2,2,512]{2,1,0:T(2,128)S(1)}, u32[]{:S(2)}, u32[]{:S(2)}) collective-permute-start(f32[2,2,512]{2,1,0:T(2,128)S(1)} %get-tuple-element.60), channel_id=1, source_target_pairs={{0,8},{8,16},{16,24},{24,0},{1,9},{9,17},{17,25},{25,1},{2,10},{10... | collective-permute-start | bytes 24584 | tf_op jit(solution)/shard_map/ppermute | solution.py:18
  73.4 9.1 %collective-permute-start.14 = (f32[2,132,2]{2,1,0:T(8,128)S(1)}, f32[2,132,2]{2,1,0:T(8,128)S(1)}, u32[]{:S(2)}, u32[]{:S(2)}) collective-permute-start(f32[2,132,2]{2,1,0:T(8,128)S(1)} %get-tuple-element.28), channel_id=1, source_target_pairs={{0,1},{1,2},{2,3},{3,4},{4,5},{5,6},{6,7},{7,0},{8,9},{9,10},{10,1... | collective-permute-start | bytes 6344 | tf_op jit(solution)/shard_map/ppermute | solution.py:18
  73.4 9.0 %collective-permute-start.15 = (f32[2,132,2]{2,1,0:T(8,128)S(1)}, f32[2,132,2]{2,1,0:T(8,128)S(1)}, u32[]{:S(2)}, u32[]{:S(2)}) collective-permute-start(f32[2,132,2]{2,1,0:T(8,128)S(1)} %get-tuple-element.29), channel_id=1, source_target_pairs={{1,0},{2,1},{3,2},{4,3},{5,4},{6,5},{7,6},{0,7},{9,8},{10,9},{11,1... | collective-permute-start | bytes 6344 | tf_op jit(solution)/shard_map/ppermute | solution.py:20
  83.8 3.1 %collective-permute-start.16 = (f32[2,2,512]{2,1,0:T(2,128)S(1)}, f32[2,2,512]{2,1,0:T(2,128)S(1)}, u32[]{:S(2)}, u32[]{:S(2)}) collective-permute-start(f32[2,2,512]{2,1,0:T(2,128)S(1)} %get-tuple-element.56), channel_id=1, source_target_pairs={{0,8},{8,16},{16,24},{24,0},{1,9},{9,17},{17,25},{25,1},{2,10},{10... | collective-permute-start | bytes 24584 | tf_op jit(solution)/shard_map/ppermute | solution.py:18
  87.0 9.0 %collective-permute-start.18 = (f32[2,132,2]{2,1,0:T(8,128)S(1)}, f32[2,132,2]{2,1,0:T(8,128)S(1)}, u32[]{:S(2)}, u32[]{:S(2)}) collective-permute-start(f32[2,132,2]{2,1,0:T(8,128)S(1)} %get-tuple-element.24), channel_id=1, source_target_pairs={{0,1},{1,2},{2,3},{3,4},{4,5},{5,6},{6,7},{7,0},{8,9},{9,10},{10,1... | collective-permute-start | bytes 6344 | tf_op jit(solution)/shard_map/ppermute | solution.py:18
  87.1 8.9 %collective-permute-start.19 = (f32[2,132,2]{2,1,0:T(8,128)S(1)}, f32[2,132,2]{2,1,0:T(8,128)S(1)}, u32[]{:S(2)}, u32[]{:S(2)}) collective-permute-start(f32[2,132,2]{2,1,0:T(8,128)S(1)} %get-tuple-element.25), channel_id=1, source_target_pairs={{1,0},{2,1},{3,2},{4,3},{5,4},{6,5},{7,6},{0,7},{9,8},{10,9},{11,1... | collective-permute-start | bytes 6344 | tf_op jit(solution)/shard_map/ppermute | solution.py:20
  97.4 3.1 %collective-permute-start.20 = (f32[2,2,512]{2,1,0:T(2,128)S(1)}, f32[2,2,512]{2,1,0:T(2,128)S(1)}, u32[]{:S(2)}, u32[]{:S(2)}) collective-permute-start(f32[2,2,512]{2,1,0:T(2,128)S(1)} %get-tuple-element.52), channel_id=1, source_target_pairs={{0,8},{8,16},{16,24},{24,0},{1,9},{9,17},{17,25},{25,1},{2,10},{10... | collective-permute-start | bytes 24584 | tf_op jit(solution)/shard_map/ppermute | solution.py:18
  100.7 9.9 %collective-permute-start.22 = (f32[2,132,2]{2,1,0:T(8,128)S(1)}, f32[2,132,2]{2,1,0:T(8,128)S(1)}, u32[]{:S(2)}, u32[]{:S(2)}) collective-permute-start(f32[2,132,2]{2,1,0:T(8,128)S(1)} %get-tuple-element.20), channel_id=1, source_target_pairs={{0,1},{1,2},{2,3},{3,4},{4,5},{5,6},{6,7},{7,0},{8,9},{9,10},{10,1... | collective-permute-start | bytes 6344 | tf_op jit(solution)/shard_map/ppermute | solution.py:18
  100.8 10.3 %collective-permute-start.23 = (f32[2,132,2]{2,1,0:T(8,128)S(1)}, f32[2,132,2]{2,1,0:T(8,128)S(1)}, u32[]{:S(2)}, u32[]{:S(2)}) collective-permute-start(f32[2,132,2]{2,1,0:T(8,128)S(1)} %get-tuple-element.21), channel_id=1, source_target_pairs={{1,0},{2,1},{3,2},{4,3},{5,4},{6,5},{7,6},{0,7},{9,8},{10,9},{11,1... | collective-permute-start | bytes 6344 | tf_op jit(solution)/shard_map/ppermute | solution.py:20
  112.4 3.1 %collective-permute-start.24 = (f32[2,2,512]{2,1,0:T(2,128)S(1)}, f32[2,2,512]{2,1,0:T(2,128)S(1)}, u32[]{:S(2)}, u32[]{:S(2)}) collective-permute-start(f32[2,2,512]{2,1,0:T(2,128)S(1)} %get-tuple-element.48), channel_id=1, source_target_pairs={{0,8},{8,16},{16,24},{24,0},{1,9},{9,17},{17,25},{25,1},{2,10},{10... | collective-permute-start | bytes 24584 | tf_op jit(solution)/shard_map/ppermute | solution.py:18
  115.7 9.0 %collective-permute-start.26 = (f32[2,132,2]{2,1,0:T(8,128)S(1)}, f32[2,132,2]{2,1,0:T(8,128)S(1)}, u32[]{:S(2)}, u32[]{:S(2)}) collective-permute-start(f32[2,132,2]{2,1,0:T(8,128)S(1)} %get-tuple-element.16), channel_id=1, source_target_pairs={{0,1},{1,2},{2,3},{3,4},{4,5},{5,6},{6,7},{7,0},{8,9},{9,10},{10,1... | collective-permute-start | bytes 6344 | tf_op jit(solution)/shard_map/ppermute | solution.py:18
  115.9 10.2 %collective-permute-start.27 = (f32[2,132,2]{2,1,0:T(8,128)S(1)}, f32[2,132,2]{2,1,0:T(8,128)S(1)}, u32[]{:S(2)}, u32[]{:S(2)}) collective-permute-start(f32[2,132,2]{2,1,0:T(8,128)S(1)} %get-tuple-element.17), channel_id=1, source_target_pairs={{1,0},{2,1},{3,2},{4,3},{5,4},{6,5},{7,6},{0,7},{9,8},{10,9},{11,1... | collective-permute-start | bytes 6344 | tf_op jit(solution)/shard_map/ppermute | solution.py:20
  127.5 3.1 %collective-permute-start.28 = (f32[2,2,512]{2,1,0:T(2,128)S(1)}, f32[2,2,512]{2,1,0:T(2,128)S(1)}, u32[]{:S(2)}, u32[]{:S(2)}) collective-permute-start(f32[2,2,512]{2,1,0:T(2,128)S(1)} %get-tuple-element.44), channel_id=1, source_target_pairs={{0,8},{8,16},{16,24},{24,0},{1,9},{9,17},{17,25},{25,1},{2,10},{10... | collective-permute-start | bytes 24584 | tf_op jit(solution)/shard_map/ppermute | solution.py:18
  130.8 9.0 %collective-permute-start.30 = (f32[2,132,2]{2,1,0:T(8,128)S(1)}, f32[2,132,2]{2,1,0:T(8,128)S(1)}, u32[]{:S(2)}, u32[]{:S(2)}) collective-permute-start(f32[2,132,2]{2,1,0:T(8,128)S(1)} %get-tuple-element.12), channel_id=1, source_target_pairs={{0,1},{1,2},{2,3},{3,4},{4,5},{5,6},{6,7},{7,0},{8,9},{9,10},{10,1... | collective-permute-start | bytes 6344 | tf_op jit(solution)/shard_map/ppermute | solution.py:18
  131.0 10.2 %collective-permute-start.31 = (f32[2,132,2]{2,1,0:T(8,128)S(1)}, f32[2,132,2]{2,1,0:T(8,128)S(1)}, u32[]{:S(2)}, u32[]{:S(2)}) collective-permute-start(f32[2,132,2]{2,1,0:T(8,128)S(1)} %get-tuple-element.13), channel_id=1, source_target_pairs={{1,0},{2,1},{3,2},{4,3},{5,4},{6,5},{7,6},{0,7},{9,8},{10,9},{11,1... | collective-permute-start | bytes 6344 | tf_op jit(solution)/shard_map/ppermute | solution.py:20
  (10 other events, 33.0 us)
